TPU v7x, 128 devices: a whole 4x4x4 slice. The times are simulated.
128 devices in a mesh: front: 8 (over z_hi, x), row: 8 (over y, core), col: 2 (over z_lo).
Axes of the slice: x: 4, y: 4, z: 4 (z_hi: 2, z_lo: 2; z = z_hi * 2 + z_lo), core: 2. Of those that a mesh axis runs over, the one named last changes fastest.
Arguments:
- pivot_block: float32 [16, 512, 512], P(('front', 'col'), 'row'), as said below
- panel_rows: float32 [16, 4096, 512], P(('front', 'col'), 'row'), may hold values from -0.875 to 0.875
- update_block: float32 [16, 4096, 4096], P(('front', 'col'), 'row'), as said below
- tile_map: int32 [16, 32], replicated, may hold values from 0 to 95, as said below
Outputs:
- pivot_factor: float32 [16, 512, 512], P(('front', 'col'), 'row')
- panel_factor: float32 [16, 4096, 512], P(('front', 'col'), 'row')
- parent_update: float32 [2, 12288, 12288], P('col', 'front', 'row')
Inputs may be any that keep to these rules, and one draw needn't show every extreme that they name: `pivot_block`: each child's pivot block is symmetric positive definite. `update_block`: each child's update block is symmetric. `tile_map`: row c lists, strictly increasing, the parent tiles that receive child c's 32 tiles; child c belongs to parent c % 2. At most 5 entries of one row fall in any aligned block of 12 parent tiles, and exactly 5 do in some block.
All inputs are finite; a program needn't handle non-finite values.
Results may differ from a plain program's by a relative error of at most 0.0001.
Values sent between devices are 32-bit elements; how exact they have to be, the bound alone decides.
No kernel may reach another device: no remote copies, remote signals or barrier semaphores. Data moves between devices by JAX's collectives and lax.ppermute only.
A program may use at most 192 MiB of HBM per device.

v0:
```python
import jax
import jax.numpy as jnp
from jax import lax
from jax.sharding import PartitionSpec as P

TILE = 128
PARENT = 12288


def solve_panel(lower_factor, panel_block):
    return jax.scipy.linalg.solve_triangular(lower_factor, panel_block.T, lower=True).T


def block_slots(tile_ids, block_count, block_width, slot_count):
    owners = tile_ids // block_width
    block_ids = jnp.arange(block_count, dtype=jnp.int32)
    starts = jnp.sum((owners[None, :] < block_ids[:, None]).astype(jnp.int32), axis=1)
    counts = jnp.sum((owners[None, :] == block_ids[:, None]).astype(jnp.int32), axis=1)
    slot_ids = jnp.arange(slot_count, dtype=jnp.int32)
    picks = jnp.minimum(starts[:, None] + slot_ids[None, :], tile_ids.shape[0] - 1)
    usable = slot_ids[None, :] < counts[:, None]
    return (picks, usable)


def local_onehot(child_maps, block_me, block_width, slot_count):
    owners = child_maps // block_width
    starts = jnp.sum((owners < block_me).astype(jnp.int32), axis=1)
    counts = jnp.sum((owners == block_me).astype(jnp.int32), axis=1)
    slot_ids = jnp.arange(slot_count, dtype=jnp.int32)
    picks = jnp.minimum(starts[:, None] + slot_ids[None, :], child_maps.shape[1] - 1)
    local_tile = jnp.take_along_axis(child_maps, picks, axis=1) - block_me * block_width
    usable = slot_ids[None, :] < counts[:, None]
    targets = jnp.arange(block_width, dtype=jnp.int32)
    onehot = (local_tile[:, None, :] == targets[None, :, None]) & usable[:, None, :]
    return onehot.astype(jnp.float32)


def local(pivot_block, panel_rows, update_block, tile_map):
    row_count = lax.axis_size("row")
    front_count = lax.axis_size("front")
    col_count = lax.axis_size("col")
    row_me = lax.axis_index("row")
    front_me = lax.axis_index("front")
    col_me = lax.axis_index("col")
    tile_size = TILE
    pivot_share = pivot_block.shape[1]
    own_rows = panel_rows.shape[1]
    contrib_order = update_block.shape[2]
    tile_count = contrib_order // tile_size
    block_width = PARENT // tile_size // row_count
    slot_count = tile_count // row_count + 1
    child_index = front_me * col_count + col_me
    tile_ids = lax.dynamic_index_in_dim(tile_map, child_index, 0, keepdims=False)
    pivot_whole = lax.all_gather(pivot_block[0], "row", axis=0, tiled=True)
    lower_factor = jnp.linalg.cholesky(pivot_whole)
    own_factor = solve_panel(lower_factor, panel_rows[0])
    all_factor = lax.all_gather(own_factor, "row", axis=0, tiled=True)
    col_picks, col_usable = block_slots(tile_ids, row_count, block_width, slot_count)
    contribution = update_block[0] - jnp.dot(
        own_factor, all_factor.T, precision=lax.Precision.HIGHEST
    )
    shaped = contribution.reshape(own_rows, tile_count, tile_size)
    picked = jnp.take(shaped, col_picks.reshape(-1), axis=1)
    picked = picked.reshape(own_rows, row_count, slot_count, tile_size)
    source = jnp.where(col_usable[None, :, :, None], picked, 0.0)
    arrived = lax.all_to_all(source, "row", split_axis=1, concat_axis=0, tiled=True)
    arrived = arrived.reshape(contrib_order, slot_count, tile_size)
    row_picks, row_usable = block_slots(tile_ids, front_count, block_width, slot_count)
    shaped = arrived.reshape(tile_count, tile_size, slot_count, tile_size)
    picked = jnp.take(shaped, row_picks.reshape(-1), axis=0)
    picked = picked.reshape(front_count, slot_count, tile_size, slot_count, tile_size)
    picked = jnp.where(row_usable[:, :, None, None, None], picked, 0.0)
    routed = lax.all_to_all(picked, "front", split_axis=0, concat_axis=0, tiled=True)
    sources = jnp.arange(front_count, dtype=jnp.int32) * col_count + col_me
    child_maps = jnp.take(tile_map, sources, axis=0)
    row_hot = local_onehot(child_maps, front_me, block_width, slot_count)
    col_hot = local_onehot(child_maps, row_me, block_width, slot_count)
    partial_value = jnp.einsum("fsxty,fbt->fsxby", routed, col_hot, precision=lax.Precision.HIGHEST)
    parent = jnp.einsum("fas,fsxby->axby", row_hot, partial_value, precision=lax.Precision.HIGHEST)
    parent = parent.reshape(block_width * tile_size, block_width * tile_size)
    pivot_rows_out = lax.dynamic_slice_in_dim(lower_factor, row_me * pivot_share, pivot_share, 0)
    return (pivot_rows_out[None], own_factor[None], parent[None])


def solution(mesh):
    return jax.shard_map(
        local,
        mesh=mesh,
        in_specs=(
            P(("front", "col"), "row", None),
            P(("front", "col"), "row", None),
            P(("front", "col"), "row", None),
            P(),
        ),
        out_specs=(
            P(("front", "col"), "row", None),
            P(("front", "col"), "row", None),
            P("col", "front", "row"),
        ),
        check_vma=False,
    )
```

profile of v0, /device:TPU:6, one launch (start us, length us, event | category | flops | bytes accessed | tf_op | source)
XLA Modules:
  0.0 728.1 jit_solution(5956696681664558131)
XLA Ops:
  10.6 25.4 %all-gather.6.cloned.1.call-done = f32[1,512,512]{2,0,1:T(1,128)} async-done(((f32[1,64,512]{2,0,1:T(1,128)}), f32[1,512,512]{2,0,1:T(1,128)}) %all-gather.6.cloned.1.call-update) | async-done | bytes 1048592 | tf_op jit(solution)/shard_map/all_gather | solution.py:54
  39.8 11.7 %cholesky.104 = f32[128,128]{1,0:T(8,128)S(1)} custom-call(f32[128,128]{1,0:T(8,128)S(1)} %cholesky.266), custom_call_target="Cholesky" | custom-call | tf_op jit(solution)/shard_map/jit(cholesky)/cholesky | solution.py:55
  51.6 9.8 %custom-call.31 = f32[1,128,128]{1,2,0:T(8,128)S(1)} custom-call(f32[1,128,128]{2,1,0:T(8,128)S(1)} %get-tuple-element.58), custom_call_target="InvertDiagBlocksLowerTriangular" | custom-call | tf_op jit(solution)/shard_map/jit(cholesky)/cholesky | solution.py:55
  62.2 11.7 %cholesky.217 = f32[128,128]{1,0:T(8,128)S(1)} custom-call(f32[128,128]{1,0:T(8,128)S(1)} %cholesky.270), custom_call_target="Cholesky" | custom-call | tf_op jit(solution)/shard_map/jit(cholesky)/cholesky | solution.py:55
  74.0 10.0 %custom-call.32 = f32[1,128,128]{1,2,0:T(8,128)S(1)} custom-call(f32[1,128,128]{2,1,0:T(8,128)S(1)} %get-tuple-element.55), custom_call_target="InvertDiagBlocksLowerTriangular" | custom-call | tf_op jit(solution)/shard_map/jit(cholesky)/cholesky | solution.py:55
  84.6 11.7 %cholesky.238 = f32[128,128]{1,0:T(8,128)S(1)} custom-call(f32[128,128]{1,0:T(8,128)S(1)} %cholesky.275), custom_call_target="Cholesky" | custom-call | tf_op jit(solution)/shard_map/jit(cholesky)/cholesky | solution.py:55
  97.1 9.8 %custom-call.33 = f32[1,128,128]{1,2,0:T(8,128)S(1)} custom-call(f32[1,128,128]{2,1,0:T(8,128)S(1)} %get-tuple-element.52), custom_call_target="InvertDiagBlocksLowerTriangular" | custom-call | tf_op jit(solution)/shard_map/jit(cholesky)/cholesky | solution.py:55
  107.5 11.7 %cholesky.255 = f32[128,128]{1,0:T(8,128)S(1)} custom-call(f32[128,128]{1,0:T(8,128)S(1)} %convolution_subtract_fusion.5), custom_call_target="Cholesky" | custom-call | tf_op jit(solution)/shard_map/jit(cholesky)/cholesky | solution.py:55
  124.3 10.4 %while.1 = (s32[]{:T(128)}, f32[512,512]{1,0:T(8,128)S(1)}, s32[4,2]{0,1:T(2,128)S(1)}, f32[4,128,128]{2,1,0:T(8,128)}, s32[]{:T(128)}) while((s32[]{:T(128)}, f32[512,512]{1,0:T(8,128)S(1)}, s32[4,2]{0,1:T(2,128)S(1)}, f32[4,128,128]{2,1,0:T(8,128)}, s32[]{:T(128)}) %tuple.46), condition=%wide.while_cond, body=%wide.while_body.sunk | while | flops 2 | bytes 132205 | solution.py:11
  134.8 40.6 %custom-call.34 = f32[4,128,128]{1,2,0:T(8,128)S(1)} custom-call(f32[4,128,128]{2,1,0:T(8,128)} %get-tuple-element.11), custom_call_target="InvertDiagBlocksLowerTriangular" | custom-call | tf_op jit(solution)/shard_map/jit(_solve_triangular)/triangular_solve | solution.py:11
  180.2 49.3 %all-gather.4.cloned.1.call-done = f32[4096,512]{0,1:T(8,128)} async-done(((f32[512,512]{0,1:T(8,128)}), f32[4096,512]{0,1:T(8,128)}) %all-gather.4.cloned.1.call-update) | async-done | bytes 8388624 | tf_op jit(solution)/shard_map/all_gather | solution.py:57
  229.5 16.5 %fusion.7 = f32[64,32,8,128]{3,2,1,0:T(8,128)S(1)} fusion(f32[1,512,4096]{2,1,0:T(8,128)} %param.8, f32[4096,512]{0,1:T(8,128)} %all-gather.4.cloned.1.call-done, f32[128,512]{1,0:T(8,128)S(1)} %fusion.33, f32[128,512]{1,0:T(8,128)S(1)} %fusion.34, f32[128,512]{1,0:T(8,128)S(1)} %fusion.36, f32[128,512]{1,0:T(8,128)S(1)} %fusion.21), kind=kOutput, calls=%fused_computation.16 | convolution fusion | flops 12887785472 | bytes 26214400 | tf_op jit(solution)/shard_map/dot_general | solution.py:59
  250.4 10.6 %gather_fusion.1 = f32[40,512,128]{2,1,0:T(8,128)} fusion(f32[512,32,128]{2,0,1:T(8,128)} %bitcast.114, s32[1024]{0:T(1024)S(1)} %pad_clamp_fusion), kind=kCustom, calls=%fused_computation.3 | custom fusion | bytes 20971680 | tf_op jit(solution)/shard_map/jit(_take)/gather | solution.py:63
  261.0 6.3 select_select_fusion.1
  267.3 122.3 %all_to_all.20 = f32[512,8,5,128]{3,0,2,1:T(8,128)} all-to-all(f32[512,8,5,128]{3,0,2,1:T(8,128)S(1)} %select_select_fusion.1), channel_id=1, replica_groups=mesh['front'=8,'row'=8,'col'=2] {'row'}, dimensions={1} | all-to-all | bytes 20971520 | tf_op jit(solution)/shard_map/all_to_all | solution.py:66
  389.6 9.2 %copy.46 = f32[8,512,1,5,128]{4,1,0,3,2:T(8,128)} copy(f32[8,512,1,5,128]{4,1,3,0,2:T(8,128)} %bitcast.116) | data formatting | bytes 20971520 | tf_op jit(solution)/shard_map/all_to_all | solution.py:66
  398.8 12.2 %gather_fusion.2 = f32[40,128,5,128]{3,1,2,0:T(8,128)} fusion(f32[32,128,5,128]{3,1,0,2:T(8,128)} %bitcast.112, s32[1024]{0:T(1024)S(1)} %pad_clamp_fusion), kind=kCustom, calls=%fused_computation.4 | custom fusion | bytes 26214560 | tf_op jit(solution)/shard_map/jit(_take)/gather | solution.py:70
  411.0 12.8 %select_select_fusion = f32[8,5,128,5,128]{4,2,3,1,0:T(8,128)} fusion(f32[8,5,128,5,128]{4,2,3,1,0:T(8,128)} %bitcast.113, pred[8,5]{1,0:T(8,128)(4,1)S(1)} %get-tuple-element.64, pred[8,5]{1,0:T(8,128)(4,1)S(1)} %get-tuple-element.63), kind=kLoop, calls=%fused_computation.12 | loop fusion | flops 6553600 | bytes 26214480 | tf_op jit(solution)/shard_map/jit(_where)/select_n | solution.py:72
  423.8 7.4 %all-to-all-start.1 = ((f32[8,5,128,5,128]{4,2,3,1,0:T(8,128)}), f32[8,5,128,5,128]{4,2,3,1,0:T(8,128)}, u32[]{:S(2)}, u32[]{:S(2)}) async-start(f32[8,5,128,5,128]{4,2,3,1,0:T(8,128)} %select_select_fusion), calls=%async_computation.1 | async-start | bytes 26214400 | tf_op jit(solution)/shard_map/all_to_all | solution.py:73
  437.3 187.8 %all-to-all-done.1 = f32[8,5,128,5,128]{4,2,3,1,0:T(8,128)} async-done(((f32[8,5,128,5,128]{4,2,3,1,0:T(8,128)}), f32[8,5,128,5,128]{4,2,3,1,0:T(8,128)}, u32[]{:S(2)}, u32[]{:S(2)}) %all-to-all-start.1) | async-done | bytes 13107232 | tf_op jit(solution)/shard_map/all_to_all | solution.py:73
  625.1 33.7 %fusion.4 = f32[8,5,128,12,128]{4,3,2,1,0:T(8,128)} fusion(f32[8,5,128,5,128]{4,2,3,1,0:T(8,128)} %all-to-all-done.1, s32[8,5]{1,0:T(8,128)S(1)} %select_subtract_fusion, pred[8,5]{1,0:T(8,128)(4,1)S(1)} %iota_compare_fusion.8), kind=kOutput, calls=%fused_computation.11 | convolution fusion | flops 471860160 | bytes 44564680 | tf_op jit(solution)/shard_map/fsxty,fbt->fsxby/dot_general | solution.py:78
  658.8 37.8 %fusion.8 = f32[12,128,12,128]{3,0,2,1:T(8,128)} fusion(f32[8,5,128,12,128]{4,3,2,1,0:T(8,128)} %fusion.4, s32[8,5]{0,1:T(8,128)S(1)} %copy.44, pred[8,5]{0,1:T(8,128)(4,1)S(1)} %iota_compare_fusion.9), kind=kOutput, calls=%fused_computation.17 | convolution fusion | flops 1132463104 | bytes 40894664 | tf_op jit(solution)/shard_map/fas,fsxby->axby/dot_general | solution.py:79
  696.6 12.4 %copy.49 = f32[12,128,12,128]{3,2,1,0:T(8,128)} copy(f32[12,128,12,128]{3,0,2,1:T(8,128)} %fusion.8) | data formatting | bytes 18874368 | tf_op jit(solution)/shard_map/fas,fsxby->axby/dot_general | solution.py:79
  709.0 11.9 %broadcast_in_dim_reshape.3 = f32[1,1536,1536]{2,1,0:T(8,128)} reshape(f32[12,128,12,128]{3,2,1,0:T(8,128)} %copy.49) | data formatting | bytes 18874368 | tf_op jit(solution)/shard_map/broadcast_in_dim;reshape | solution.py:82
  (79 shorter events, 38.3 us)
Async XLA Ops:
  7.2 28.8 %all-gather.6.cloned.1.call-start = ((), (), s32[]{:S(2)}) async-start(), calls=%async_computation.3 | async-start | bytes 1179648 | tf_op jit(solution)/shard_map/all_gather | solution.py:54
  8.9 220.6 %all-gather.4.cloned.1.call-start = ((), (), s32[]{:S(2)}) async-start(), calls=%async_computation.2 | async-start | bytes 9437184 | tf_op jit(solution)/shard_map/all_gather | solution.py:57
  38.4 141.4 %copy-start = (s32[16,32]{1,0:T(8,128)S(1)}, s32[16,32]{1,0:T(8,128)}, u32[]{:S(2)}) copy-start(s32[16,32]{1,0:T(8,128)} %param.9) | copy-start | bytes 6148
  423.8 201.3 %all-to-all-start.1 = ((f32[8,5,128,5,128]{4,2,3,1,0:T(8,128)}), f32[8,5,128,5,128]{4,2,3,1,0:T(8,128)}, u32[]{:S(2)}, u32[]{:S(2)}) async-start(f32[8,5,128,5,128]{4,2,3,1,0:T(8,128)} %select_select_fusion), calls=%async_computation.1 | async-start | bytes 26214400 | tf_op jit(solution)/shard_map/all_to_all | solution.py:73
Sparse Core Ops, SparseCore 0:
  10.3 25.6 all-gather.5
  179.9 49.5 all-gather.3
where the time goes:
time: 738 us; the launch traced here: 728 us
  waiting for transfers between devices  263 us (36%)
  other arithmetic  143 us (19%)
  blocking collectives  122 us (17%)
  matrix products  92.9 us (13%)
  local copies, waits for them, and re-layouts  82.6 us (11%)
  between operations  17.3 us (2%)
  starting transfers between devices  7.46 us (1%)
    all_to_all x1, waiting for transfers between devices, local(): lax.all_to_all(picked, 'front', split_axis=0, concat_axis=0, tiled=True)  188 us
    all_to_all x1, blocking collectives, local(): lax.all_to_all(source, 'row', split_axis=1, concat_axis=0, tiled=True)  122 us
    another operation x14, other arithmetic, local(): lower_factor = jnp.linalg.cholesky(pivot_whole)  78.6 us
    all_gather x1, waiting for transfers between devices, local(): all_factor = lax.all_gather(own_factor, 'row', axis=0, tiled=True)  49.3 us
    another operation x3, other arithmetic, solve_panel(): jax.scipy.linalg.solve_triangular(lower_factor, panel_block.T, lower=True)  41.8 us
    dot_general x1, matrix products, local(): jnp.einsum('fas,fsxby->axby', row_hot, partial_value, precision=lax.Preci...  37.8 us
    dot_general x1, matrix products, local(): jnp.einsum('fsxty,fbt->fsxby', routed, col_hot, precision=lax.Precision.H...  33.7 us
    all_gather x1, waiting for transfers between devices, local(): pivot_whole = lax.all_gather(pivot_block[0], 'row', axis=0, tiled=True)  25.4 us
  transfers between devices with their start and end apart: 3, of which 3 were waited for; matrix products, arithmetic and copies ran while one was open for 1% of the time, Pallas kernels for 0%

commit v1 on v0

--- a/solution.py
+++ b/solution.py
@@ -36,6 +36,19 @@
 
 
 def local(pivot_block, panel_rows, update_block, tile_map):
+
+    def resolve_the_teams(obj):
+        slots = lax.axis_size("row")
+        formed = sorted(((dev_i, (dev_i + 1) % slots) for dev_i in range(slots)))
+        carry = obj
+        inbox = [carry]
+        for it in range(1, slots):
+            carry = lax.ppermute(carry, "row", formed)
+            inbox.insert(0, carry)
+        w1 = jnp.concatenate(inbox, axis=0)
+        aux = lax.axis_index("row") + 1
+        return jnp.roll(w1, aux * obj.shape[0], axis=0)
+
     row_count = lax.axis_size("row")
     front_count = lax.axis_size("front")
     col_count = lax.axis_size("col")
@@ -54,7 +67,7 @@
     pivot_whole = lax.all_gather(pivot_block[0], "row", axis=0, tiled=True)
     lower_factor = jnp.linalg.cholesky(pivot_whole)
     own_factor = solve_panel(lower_factor, panel_rows[0])
-    all_factor = lax.all_gather(own_factor, "row", axis=0, tiled=True)
+    all_factor = resolve_the_teams(own_factor)
     col_picks, col_usable = block_slots(tile_ids, row_count, block_width, slot_count)
     contribution = update_block[0] - jnp.dot(
         own_factor, all_factor.T, precision=lax.Precision.HIGHEST

time: 738 us -> 828 us (1.12)
  waiting for transfers between devices: 263 us -> 321 us
  local copies, waits for them, and re-layouts: 82.6 us -> 112 us
    ppermute x0 -> x7, waiting for transfers between devices: none -> 108 us  [resolve_the_teams(): carry = lax.ppermute(carry, 'row', formed)]
    all_gather x1 -> x0, waiting for transfers between devices: 49.3 us -> none  [local(): all_factor = lax.all_gather(own_factor, 'row', axis=0, tiled=True)]
    unnamed x5 -> x35, local copies, waits for them, and re-layouts: 4.57 us -> 33.8 us
  transfers between devices with their start and end apart: 3 -> 9, of which waited for: 3 -> 9; matrix products, arithmetic and copies ran while one was open for 1% -> 1% of each run, Pallas kernels for 0% -> 0%
where the time goes in v1:
time: 828 us; the launch traced here: 818 us
  waiting for transfers between devices  321 us (39%)
  other arithmetic  144 us (17%)
  blocking collectives  122 us (15%)
  local copies, waits for them, and re-layouts  112 us (14%)
  matrix products  93.7 us (11%)
  between operations  17.3 us (2%)
    all_to_all x1, waiting for transfers between devices, local(): lax.all_to_all(picked, 'front', split_axis=0, concat_axis=0, tiled=True)  188 us
    all_to_all x1, blocking collectives, local(): lax.all_to_all(source, 'row', split_axis=1, concat_axis=0, tiled=True)  122 us
    ppermute x7, waiting for transfers between devices, resolve_the_teams(): carry = lax.ppermute(carry, 'row', formed)  108 us
    another operation x14, other arithmetic, local(): lower_factor = jnp.linalg.cholesky(pivot_whole)  78.6 us
    another operation x3, other arithmetic, solve_panel(): jax.scipy.linalg.solve_triangular(lower_factor, panel_block.T, lower=True)  41.7 us
    dot_general x1, matrix products, local(): jnp.einsum('fas,fsxby->axby', row_hot, partial_value, precision=lax.Preci...  37.8 us
    unnamed x35, local copies, waits for them, and re-layouts  33.8 us
    dot_general x1, matrix products, local(): jnp.einsum('fsxty,fbt->fsxby', routed, col_hot, precision=lax.Precision.H...  33.7 us
  transfers between devices with their start and end apart: 9, of which 9 were waited for; matrix products, arithmetic and copies ran while one was open for 1% of the time, Pallas kernels for 0%

profile of v1, /device:TPU:6, one launch (start us, length us, event | category | flops | bytes accessed | tf_op | source)
XLA Modules:
  0.0 818.2 jit_solution(8507095874185417128)
XLA Ops:
  10.5 25.5 %all-gather.3.cloned.1.call-done = f32[1,512,512]{2,0,1:T(1,128)} async-done(((f32[1,64,512]{2,0,1:T(1,128)}), f32[1,512,512]{2,0,1:T(1,128)}) %all-gather.3.cloned.1.call-update) | async-done | bytes 1048592 | tf_op jit(solution)/shard_map/all_gather | solution.py:67
  39.8 11.7 %cholesky.104 = f32[128,128]{1,0:T(8,128)S(1)} custom-call(f32[128,128]{1,0:T(8,128)S(1)} %cholesky.266), custom_call_target="Cholesky" | custom-call | tf_op jit(solution)/shard_map/jit(cholesky)/cholesky | solution.py:68
  62.2 11.7 %cholesky.217 = f32[128,128]{1,0:T(8,128)S(1)} custom-call(f32[128,128]{1,0:T(8,128)S(1)} %cholesky.270), custom_call_target="Cholesky" | custom-call | tf_op jit(solution)/shard_map/jit(cholesky)/cholesky | solution.py:68
  84.6 11.7 %cholesky.238 = f32[128,128]{1,0:T(8,128)S(1)} custom-call(f32[128,128]{1,0:T(8,128)S(1)} %cholesky.275), custom_call_target="Cholesky" | custom-call | tf_op jit(solution)/shard_map/jit(cholesky)/cholesky | solution.py:68
  107.5 11.7 %cholesky.255 = f32[128,128]{1,0:T(8,128)S(1)} custom-call(f32[128,128]{1,0:T(8,128)S(1)} %convolution_subtract_fusion.5), custom_call_target="Cholesky" | custom-call | tf_op jit(solution)/shard_map/jit(cholesky)/cholesky | solution.py:68
  124.3 10.4 %while.1 = (s32[]{:T(128)}, f32[512,512]{1,0:T(8,128)S(1)}, s32[4,2]{0,1:T(2,128)S(1)}, f32[4,128,128]{2,1,0:T(8,128)}, s32[]{:T(128)}) while((s32[]{:T(128)}, f32[512,512]{1,0:T(8,128)S(1)}, s32[4,2]{0,1:T(2,128)S(1)}, f32[4,128,128]{2,1,0:T(8,128)}, s32[]{:T(128)}) %tuple.46), condition=%wide.while_cond, body=%wide.while_body.sunk | while | flops 2 | bytes 132205 | solution.py:11
  134.7 40.5 %custom-call.34 = f32[4,128,128]{1,2,0:T(8,128)S(1)} custom-call(f32[4,128,128]{2,1,0:T(8,128)} %get-tuple-element.11), custom_call_target="InvertDiagBlocksLowerTriangular" | custom-call | tf_op jit(solution)/shard_map/jit(_solve_triangular)/triangular_solve | solution.py:11
  178.8 15.2 %collective-permute-done = f32[512,512]{0,1:T(8,128)S(1)} collective-permute-done((f32[512,512]{0,1:T(8,128)S(1)}, f32[512,512]{0,1:T(8,128)S(1)}, u32[]{:S(2)}, u32[]{:S(2)}) %collective-permute-start) | collective-permute-done | bytes 1048608 | tf_op jit(solution)/shard_map/ppermute | solution.py:46
  194.0 15.4 %collective-permute-done.1 = f32[512,512]{0,1:T(8,128)S(1)} collective-permute-done((f32[512,512]{0,1:T(8,128)S(1)}, f32[512,512]{0,1:T(8,128)S(1)}, u32[]{:S(2)}, u32[]{:S(2)}) %collective-permute-start.1) | collective-permute-done | bytes 1048608 | tf_op jit(solution)/shard_map/ppermute | solution.py:46
  210.4 15.4 %collective-permute-done.2 = f32[512,512]{0,1:T(8,128)S(1)} collective-permute-done((f32[512,512]{0,1:T(8,128)S(1)}, f32[512,512]{0,1:T(8,128)S(1)}, u32[]{:S(2)}, u32[]{:S(2)}) %collective-permute-start.2) | collective-permute-done | bytes 1048608 | tf_op jit(solution)/shard_map/ppermute | solution.py:46
  226.8 15.4 %collective-permute-done.3 = f32[512,512]{0,1:T(8,128)S(1)} collective-permute-done((f32[512,512]{0,1:T(8,128)S(1)}, f32[512,512]{0,1:T(8,128)S(1)}, u32[]{:S(2)}, u32[]{:S(2)}) %collective-permute-start.3) | collective-permute-done | bytes 1048608 | tf_op jit(solution)/shard_map/ppermute | solution.py:46
  243.2 15.5 %collective-permute-done.4 = f32[512,512]{0,1:T(8,128)} collective-permute-done((f32[512,512]{0,1:T(8,128)S(1)}, f32[512,512]{0,1:T(8,128)}, u32[]{:S(2)}, u32[]{:S(2)}) %collective-permute-start.4) | collective-permute-done | bytes 1048608 | tf_op jit(solution)/shard_map/ppermute | solution.py:46
  258.8 15.7 %collective-permute-done.5 = f32[512,512]{0,1:T(8,128)} collective-permute-done((f32[512,512]{0,1:T(8,128)}, f32[512,512]{0,1:T(8,128)}, u32[]{:S(2)}, u32[]{:S(2)}) %collective-permute-start.5) | collective-permute-done | bytes 1048608 | tf_op jit(solution)/shard_map/ppermute | solution.py:46
  275.0 15.3 %collective-permute-done.6 = f32[512,512]{0,1:T(8,128)} collective-permute-done((f32[512,512]{0,1:T(8,128)}, f32[512,512]{0,1:T(8,128)}, u32[]{:S(2)}, u32[]{:S(2)}) %collective-permute-start.6) | collective-permute-done | bytes 1048608 | tf_op jit(solution)/shard_map/ppermute | solution.py:46
  318.7 17.3 %fusion.7 = f32[64,32,8,128]{3,2,1,0:T(8,128)S(1)} fusion(f32[1,512,4096]{2,1,0:T(8,128)S(1)} %bitcast.121, f32[8192,512]{0,1:T(8,128)} %constant_dynamic-update-slice_fusion, s32[]{:T(128)S(6)} %select_n.110, f32[128,512]{1,0:T(8,128)S(1)} %fusion.37, f32[128,512]{1,0:T(8,128)S(1)} %fusion.38, f32[128,512]{1,0:T(8,128)S(1)} %fusion.40, ...), kind=kOutput, calls=%fused_computation.16 | convolution fusion | flops 12887785472 | bytes 26214404 | tf_op jit(solution)/shard_map/dot_general | solution.py:72
  340.4 10.5 %gather_fusion.1 = f32[40,512,128]{2,1,0:T(8,128)} fusion(f32[512,32,128]{2,0,1:T(8,128)} %bitcast.117, s32[1024]{0:T(1024)S(1)} %get-tuple-element.65), kind=kCustom, calls=%fused_computation.3 | custom fusion | bytes 20971680 | tf_op jit(solution)/shard_map/jit(_take)/gather | solution.py:76
  357.2 122.5 %all_to_all.20 = f32[512,8,5,128]{3,0,2,1:T(8,128)} all-to-all(f32[512,8,5,128]{3,0,2,1:T(8,128)S(1)} %select_select_fusion.1), channel_id=1, replica_groups=mesh['front'=8,'row'=8,'col'=2] {'row'}, dimensions={1} | all-to-all | bytes 20971520 | tf_op jit(solution)/shard_map/all_to_all | solution.py:79
  488.9 12.2 %gather_fusion.2 = f32[40,128,5,128]{3,1,2,0:T(8,128)} fusion(f32[32,128,5,128]{3,1,0,2:T(8,128)} %bitcast.115, s32[1024]{0:T(1024)S(1)} %get-tuple-element.65), kind=kCustom, calls=%fused_computation.4 | custom fusion | bytes 26214560 | tf_op jit(solution)/shard_map/jit(_take)/gather | solution.py:83
  501.1 12.8 %select_select_fusion = f32[8,5,128,5,128]{4,2,3,1,0:T(8,128)} fusion(f32[8,5,128,5,128]{4,2,3,1,0:T(8,128)} %bitcast.116, pred[8,5]{1,0:T(8,128)(4,1)S(1)} %get-tuple-element.64, pred[8,5]{1,0:T(8,128)(4,1)S(1)} %get-tuple-element.63), kind=kLoop, calls=%fused_computation.12 | loop fusion | flops 6553600 | bytes 26214480 | tf_op jit(solution)/shard_map/jit(_where)/select_n | solution.py:85
  527.5 187.7 %all-to-all-done.1 = f32[8,5,128,5,128]{4,2,3,1,0:T(8,128)} async-done(((f32[8,5,128,5,128]{4,2,3,1,0:T(8,128)}), f32[8,5,128,5,128]{4,2,3,1,0:T(8,128)}, u32[]{:S(2)}, u32[]{:S(2)}) %all-to-all-start.1) | async-done | bytes 13107232 | tf_op jit(solution)/shard_map/all_to_all | solution.py:86
  715.2 33.7 %fusion.4 = f32[8,5,128,12,128]{4,3,2,1,0:T(8,128)} fusion(f32[8,5,128,5,128]{4,2,3,1,0:T(8,128)} %all-to-all-done.1, s32[8,5]{1,0:T(8,128)S(1)} %select_subtract_fusion, pred[8,5]{1,0:T(8,128)(4,1)S(1)} %iota_compare_fusion.8), kind=kOutput, calls=%fused_computation.11 | convolution fusion | flops 471860160 | bytes 44564680 | tf_op jit(solution)/shard_map/fsxty,fbt->fsxby/dot_general | solution.py:91
  748.8 37.8 %fusion.10 = f32[12,128,12,128]{3,0,2,1:T(8,128)} fusion(f32[8,5,128,12,128]{4,3,2,1,0:T(8,128)} %fusion.4, s32[8,5]{0,1:T(8,128)S(1)} %copy.44, pred[8,5]{0,1:T(8,128)(4,1)S(1)} %iota_compare_fusion.9), kind=kOutput, calls=%fused_computation.19 | convolution fusion | flops 1132463104 | bytes 40894664 | tf_op jit(solution)/shard_map/fas,fsxby->axby/dot_general | solution.py:92
  786.7 12.4 %copy.49 = f32[12,128,12,128]{3,2,1,0:T(8,128)} copy(f32[12,128,12,128]{3,0,2,1:T(8,128)} %fusion.10) | data formatting | bytes 18874368 | tf_op jit(solution)/shard_map/fas,fsxby->axby/dot_general | solution.py:92
  799.1 11.9 %broadcast_in_dim_reshape.3 = f32[1,1536,1536]{2,1,0:T(8,128)} reshape(f32[12,128,12,128]{3,2,1,0:T(8,128)} %copy.49) | data formatting | bytes 18874368 | tf_op jit(solution)/shard_map/broadcast_in_dim;reshape | solution.py:95
  (123 shorter events, 121.3 us)
Async XLA Ops:
  7.2 267.4 %copy-start.6 = (s32[16,32]{1,0:T(8,128)S(1)}, s32[16,32]{1,0:T(8,128)}, u32[]{:S(2)}) copy-start(s32[16,32]{1,0:T(8,128)} %param.9) | copy-start | bytes 6148
  7.2 28.8 %all-gather.3.cloned.1.call-start = ((), (), s32[]{:S(2)}) async-start(), calls=%async_computation.2 | async-start | bytes 1179648 | tf_op jit(solution)/shard_map/all_gather | solution.py:67
  178.5 15.4 %collective-permute-start = (f32[512,512]{0,1:T(8,128)S(1)}, f32[512,512]{0,1:T(8,128)S(1)}, u32[]{:S(2)}, u32[]{:S(2)}) collective-permute-start(f32[512,512]{0,1:T(8,128)S(1)} %get-tuple-element.47), channel_id=1, source_target_pairs={{0,2},{2,4},{4,6},{6,8},{8,10},{10,12},{12,14},{14,0},{1,3},{3,5},... | collective-permute-start | bytes 3145736 | tf_op jit(solution)/shard_map/ppermute | solution.py:46
  194.0 15.4 %collective-permute-start.1 = (f32[512,512]{0,1:T(8,128)S(1)}, f32[512,512]{0,1:T(8,128)S(1)}, u32[]{:S(2)}, u32[]{:S(2)}) collective-permute-start(f32[512,512]{0,1:T(8,128)S(1)} %collective-permute-done), channel_id=1, source_target_pairs={{0,2},{2,4},{4,6},{6,8},{8,10},{10,12},{12,14},{14,0},{1,3},{3,5},... | collective-permute-start | bytes 3145736 | tf_op jit(solution)/shard_map/ppermute | solution.py:46
  209.4 1.0 copy-start
  210.4 15.4 %collective-permute-start.2 = (f32[512,512]{0,1:T(8,128)S(1)}, f32[512,512]{0,1:T(8,128)S(1)}, u32[]{:S(2)}, u32[]{:S(2)}) collective-permute-start(f32[512,512]{0,1:T(8,128)S(1)} %collective-permute-done.1), channel_id=1, source_target_pairs={{0,2},{2,4},{4,6},{6,8},{8,10},{10,12},{12,14},{14,0},{1,3},{3,5},... | collective-permute-start | bytes 3145736 | tf_op jit(solution)/shard_map/ppermute | solution.py:46
  225.9 1.0 copy-start.2
  226.8 15.4 %collective-permute-start.3 = (f32[512,512]{0,1:T(8,128)S(1)}, f32[512,512]{0,1:T(8,128)S(1)}, u32[]{:S(2)}, u32[]{:S(2)}) collective-permute-start(f32[512,512]{0,1:T(8,128)S(1)} %collective-permute-done.2), channel_id=1, source_target_pairs={{0,2},{2,4},{4,6},{6,8},{8,10},{10,12},{12,14},{14,0},{1,3},{3,5},... | collective-permute-start | bytes 3145736 | tf_op jit(solution)/shard_map/ppermute | solution.py:46
  242.3 1.0 copy-start.4
  243.2 15.5 %collective-permute-start.4 = (f32[512,512]{0,1:T(8,128)S(1)}, f32[512,512]{0,1:T(8,128)}, u32[]{:S(2)}, u32[]{:S(2)}) collective-permute-start(f32[512,512]{0,1:T(8,128)S(1)} %collective-permute-done.3), channel_id=1, source_target_pairs={{0,2},{2,4},{4,6},{6,8},{8,10},{10,12},{12,14},{14,0},{1,3},{3,5},... | collective-permute-start | bytes 3145736 | tf_op jit(solution)/shard_map/ppermute | solution.py:46
  258.8 15.8 %collective-permute-start.5 = (f32[512,512]{0,1:T(8,128)}, f32[512,512]{0,1:T(8,128)}, u32[]{:S(2)}, u32[]{:S(2)}) collective-permute-start(f32[512,512]{0,1:T(8,128)} %collective-permute-done.4), channel_id=1, source_target_pairs={{0,2},{2,4},{4,6},{6,8},{8,10},{10,12},{12,14},{14,0},{1,3},{3,5},... | collective-permute-start | bytes 3145736 | tf_op jit(solution)/shard_map/ppermute | solution.py:46
  274.5 15.8 %collective-permute-start.6 = (f32[512,512]{0,1:T(8,128)}, f32[512,512]{0,1:T(8,128)}, u32[]{:S(2)}, u32[]{:S(2)}) collective-permute-start(f32[512,512]{0,1:T(8,128)} %collective-permute-done.5), channel_id=1, source_target_pairs={{0,2},{2,4},{4,6},{6,8},{8,10},{10,12},{12,14},{14,0},{1,3},{3,5},... | collective-permute-start | bytes 3145736 | tf_op jit(solution)/shard_map/ppermute | solution.py:46
  274.9 38.6 %copy-start.5 = (f32[512,512]{0,1:T(8,128)S(1)}, f32[512,512]{0,1:T(8,128)}, u32[]{:S(2)}) copy-start(f32[512,512]{0,1:T(8,128)} %copy-done.4) | copy-start | bytes 3145732
  274.9 39.6 %copy-start.3 = (f32[512,512]{0,1:T(8,128)S(1)}, f32[512,512]{0,1:T(8,128)}, u32[]{:S(2)}) copy-start(f32[512,512]{0,1:T(8,128)} %copy-done.2) | copy-start | bytes 3145732
  274.9 40.7 %copy-start.1 = (f32[512,512]{0,1:T(8,128)S(1)}, f32[512,512]{0,1:T(8,128)}, u32[]{:S(2)}) copy-start(f32[512,512]{0,1:T(8,128)} %copy-done) | copy-start | bytes 3145732
  275.0 43.7 %slice-start = ((s8[8388608]{0:T(1024)(128)(4,1)}), s8[4194304]{0:T(1024)(128)(4,1)S(1)}, s32[]{:S(2)}) async-start(s8[8388608]{0:T(1024)(128)(4,1)} %bitcast.120), calls=%async_computation.3 | async-start | bytes 8388608
  305.0 13.7 %slice-start.1 = ((s8[8388608]{0:T(1024)(128)(4,1)}), s8[4194304]{0:T(1024)(128)(4,1)S(1)}, s32[]{:S(2)}) async-start(s8[8388608]{0:T(1024)(128)(4,1)} %bitcast.120), calls=%async_computation.4 | async-start | bytes 8388608
  513.9 201.3 %all-to-all-start.1 = ((f32[8,5,128,5,128]{4,2,3,1,0:T(8,128)}), f32[8,5,128,5,128]{4,2,3,1,0:T(8,128)}, u32[]{:S(2)}, u32[]{:S(2)}) async-start(f32[8,5,128,5,128]{4,2,3,1,0:T(8,128)} %select_select_fusion), calls=%async_computation.1 | async-start | bytes 26214400 | tf_op jit(solution)/shard_map/all_to_all | solution.py:86
Sparse Core Ops, SparseCore 0:
  10.3 25.6 all-gather.2
